TPU v7x, 512 devices: a whole 4x4x16 slice. The times are simulated.
512 devices in a mesh: tm: 128 (over z, y, core), chan: 4 (over x).
Axes of the slice: x: 4, y: 4, z: 16, core: 2. Of those that a mesh axis runs over, the one named last changes fastest.
Arguments:
- markov: float32 [16384, 256, 4], P('tm', 'chan'), may hold values from -6 to 6
- sketch: float32 [16384, 4, 64], P('tm'), may hold values from -0.0234375 to 0.0234375
Outputs:
- basis: float32 [16384, 256, 64], P('tm', 'chan')
- factor: float32 [64, 64], replicated
All inputs are finite; a program needn't handle non-finite values.
Results may differ from a plain program's by a relative error of at most 0.000098.
Values sent between devices are 32-bit elements; how exact they have to be, the bound alone decides.
A program may use at most 128 MiB of HBM per device.

v0:
```python
import math
import jax
import jax.numpy as jnp
from jax import lax
from jax.sharding import PartitionSpec as P

HIGHEST_PREC = lax.Precision.HIGHEST


def circle(first, second, modulus):
    angle = (first[:, None] * second[None, :] % modulus).astype(jnp.float32) * (
        2.0 * math.pi / modulus
    )
    return (jnp.cos(angle), jnp.sin(angle))


def matmul_rows(matrix, blocks):
    return jnp.einsum("ab,bgw->agw", matrix, blocks, precision=HIGHEST_PREC)


def plain_dot(left, right):
    return jnp.dot(left, right, precision=HIGHEST_PREC)


def gram_of(matrix):
    return jnp.einsum("nr,ns->rs", matrix, matrix, precision=HIGHEST_PREC)


def product(left, right):
    return jnp.einsum("kpm,kmr->kpr", left, right, precision=HIGHEST_PREC)


def total_factor(gram_part, row_total):
    summed = lax.psum(gram_part, ("tm", "chan"))
    result = jnp.linalg.cholesky(summed / row_total)
    return result


def body(markov, sketch):
    seq_len = markov.shape[0]
    shards = lax.axis_size("tm")
    per_group = seq_len // shards
    whole_len = seq_len * shards
    own_index = lax.axis_index("tm")
    channels = markov.shape[1]
    inputs = markov.shape[2]
    columns = sketch.shape[2]
    row_total = whole_len * channels * lax.axis_size("chan")
    small_index = jnp.arange(shards, dtype=jnp.int32)
    time_index = jnp.arange(seq_len, dtype=jnp.int32)
    freq_index = own_index + shards * time_index
    cos_small, sin_small = circle(small_index, small_index, shards)
    cos_large, sin_large = circle(freq_index, time_index, whole_len)
    markov_blocks = markov.reshape(shards, per_group, channels * inputs)
    sketch_blocks = sketch.reshape(shards, per_group, inputs * columns)
    pieces = (
        lax.all_to_all(markov_blocks, "tm", split_axis=0, concat_axis=0, tiled=True),
        lax.all_to_all(sketch_blocks, "tm", split_axis=0, concat_axis=0, tiled=True),
    )
    results = []
    for piece_block in pieces:
        results.append(matmul_rows(cos_small, piece_block))
        results.append(-matmul_rows(sin_small, piece_block))
    spread = tuple(results)
    pieces = (
        lax.all_to_all(spread[0], "tm", split_axis=0, concat_axis=1, tiled=True),
        lax.all_to_all(spread[1], "tm", split_axis=0, concat_axis=1, tiled=True),
        lax.all_to_all(spread[2], "tm", split_axis=0, concat_axis=1, tiled=True),
        lax.all_to_all(spread[3], "tm", split_axis=0, concat_axis=1, tiled=True),
    )
    results = []
    for place in range(0, len(pieces), 2):
        real_part = pieces[place].reshape(seq_len, -1)
        imag_part = pieces[place + 1].reshape(seq_len, -1)
        results.append(plain_dot(cos_large, real_part) + plain_dot(sin_large, imag_part))
        results.append(plain_dot(cos_large, imag_part) - plain_dot(sin_large, real_part))
    markov_re, markov_im, sketch_re, sketch_im = tuple(results)
    markov_re = markov_re.reshape(seq_len, channels, inputs)
    markov_im = markov_im.reshape(seq_len, channels, inputs)
    sketch_re = sketch_re.reshape(seq_len, inputs, columns)
    sketch_im = sketch_im.reshape(seq_len, inputs, columns)
    spec_re = (product(markov_re, sketch_re) + product(markov_im, sketch_im)).reshape(
        seq_len * channels, columns
    )
    spec_im = (product(markov_im, sketch_re) - product(markov_re, sketch_im)).reshape(
        seq_len * channels, columns
    )
    identity_m = jnp.eye(columns, dtype=jnp.float32)
    real_part = spec_re.reshape(seq_len, channels * columns)
    imag_part = spec_im.reshape(seq_len, channels * columns)
    width = real_part.shape[1]
    turned_re = plain_dot(cos_large.T, real_part) - plain_dot(sin_large.T, imag_part)
    turned_im = plain_dot(sin_large.T, real_part) + plain_dot(cos_large.T, imag_part)
    pieces = (
        lax.all_to_all(
            turned_re.reshape(shards, per_group, width),
            "tm",
            split_axis=0,
            concat_axis=0,
            tiled=True,
        ),
        lax.all_to_all(
            turned_im.reshape(shards, per_group, width),
            "tm",
            split_axis=0,
            concat_axis=0,
            tiled=True,
        ),
    )
    mixed = (matmul_rows(cos_small, pieces[0]) - matmul_rows(sin_small, pieces[1])) / whole_len
    returned = lax.all_to_all(mixed, "tm", split_axis=0, concat_axis=1, tiled=True)
    result_time = returned.reshape(seq_len, width)
    signal = result_time
    signal = signal.reshape(seq_len * channels, columns)
    gram_part = gram_of(signal)
    lower_factor = total_factor(gram_part, row_total)
    inverse_t = jax.scipy.linalg.solve_triangular(lower_factor, identity_m, lower=True).T
    result = plain_dot(signal, inverse_t)
    return (result.reshape(seq_len, channels, columns), lower_factor.T)


def solution(mesh):
    return jax.shard_map(
        body,
        mesh=mesh,
        in_specs=(P("tm", "chan", None), P("tm", None, None)),
        out_specs=(P("tm", "chan", None), P()),
        check_vma=False,
    )
```

profile of v0, /device:TPU:1, one launch (start us, length us, event | category | flops | bytes accessed | tf_op | source)
XLA Modules:
  0.0 682.6 jit_solution(10656477915658200802)
XLA Ops:
  0.6 1.7 copy.57
  2.3 20.6 %all-to-all-start = ((f32[128,1,256]{2,1,0:T(1,128)}), f32[128,1,256]{2,1,0:T(1,128)S(1)}, u32[]{:S(2)}, u32[]{:S(2)}) async-start(f32[128,1,256]{2,1,0:T(1,128)} %copy.57), calls=%async_computation | async-start | bytes 262144 | tf_op jit(solution)/shard_map/all_to_all | solution.py:57
  22.8 1.7 copy.61
  24.5 14.3 %all-to-all-done = f32[128,1,256]{2,1,0:T(1,128)S(1)} async-done(((f32[128,1,256]{2,1,0:T(1,128)}), f32[128,1,256]{2,1,0:T(1,128)S(1)}, u32[]{:S(2)}, u32[]{:S(2)}) %all-to-all-start) | async-done | bytes 131104 | tf_op jit(solution)/shard_map/all_to_all | solution.py:57
  38.8 7.2 %all-to-all-start.3 = ((f32[128,1,256]{2,1,0:T(1,128)}), f32[128,1,256]{2,1,0:T(1,128)S(1)}, u32[]{:S(2)}, u32[]{:S(2)}) async-start(f32[128,1,256]{2,1,0:T(1,128)} %copy.61), calls=%async_computation.3 | async-start | bytes 262144 | tf_op jit(solution)/shard_map/all_to_all | solution.py:58
  46.1 0.5 fusion.10
  46.6 0.8 copy.59
  47.4 14.6 %all-to-all-done.3 = f32[128,1,256]{2,1,0:T(1,128)S(1)} async-done(((f32[128,1,256]{2,1,0:T(1,128)}), f32[128,1,256]{2,1,0:T(1,128)S(1)}, u32[]{:S(2)}, u32[]{:S(2)}) %all-to-all-start.3) | async-done | bytes 131104 | tf_op jit(solution)/shard_map/all_to_all | solution.py:58
  62.0 7.3 %all-to-all-start.2 = ((f32[128,1,256]{2,1,0:T(1,128)}), f32[128,1,256]{2,1,0:T(1,128)S(1)}, u32[]{:S(2)}, u32[]{:S(2)}) async-start(f32[128,1,256]{2,1,0:T(1,128)} %copy.59), calls=%async_computation.2 | async-start | bytes 262144 | tf_op jit(solution)/shard_map/all_to_all | solution.py:67
  69.3 0.5 convolution_bitcast_fusion.1
  69.8 0.8 copy.58
  70.6 14.7 %all-to-all-done.2 = f32[128,1,256]{2,1,0:T(1,128)S(1)} async-done(((f32[128,1,256]{2,1,0:T(1,128)}), f32[128,1,256]{2,1,0:T(1,128)S(1)}, u32[]{:S(2)}, u32[]{:S(2)}) %all-to-all-start.2) | async-done | bytes 131104 | tf_op jit(solution)/shard_map/all_to_all | solution.py:67
  85.2 7.2 %all-to-all-start.1 = ((f32[128,1,256]{2,1,0:T(1,128)}), f32[128,1,256]{2,1,0:T(1,128)S(1)}, u32[]{:S(2)}, u32[]{:S(2)}) async-start(f32[128,1,256]{2,1,0:T(1,128)} %copy.58), calls=%async_computation.1 | async-start | bytes 262144 | tf_op jit(solution)/shard_map/all_to_all | solution.py:66
  92.5 0.5 fusion.9
  93.0 0.8 copy.63
  93.8 14.7 %all-to-all-done.1 = f32[128,1,256]{2,1,0:T(1,128)S(1)} async-done(((f32[128,1,256]{2,1,0:T(1,128)}), f32[128,1,256]{2,1,0:T(1,128)S(1)}, u32[]{:S(2)}, u32[]{:S(2)}) %all-to-all-start.1) | async-done | bytes 131104 | tf_op jit(solution)/shard_map/all_to_all | solution.py:66
  108.5 7.7 %all-to-all-start.5 = ((f32[128,1,256]{2,1,0:T(1,128)}), f32[128,1,256]{2,1,0:T(1,128)S(1)}, u32[]{:S(2)}, u32[]{:S(2)}) async-start(f32[128,1,256]{2,1,0:T(1,128)} %copy.63), calls=%async_computation.5 | async-start | bytes 262144 | tf_op jit(solution)/shard_map/all_to_all | solution.py:69
  116.1 0.5 convolution_bitcast_fusion
  116.6 0.8 copy.62
  117.4 0.6 fusion.19
  118.0 0.6 convolution_subtract_fusion.4
  118.6 13.5 %all-to-all-done.5 = f32[128,1,256]{2,1,0:T(1,128)S(1)} async-done(((f32[128,1,256]{2,1,0:T(1,128)}), f32[128,1,256]{2,1,0:T(1,128)S(1)}, u32[]{:S(2)}, u32[]{:S(2)}) %all-to-all-start.5) | async-done | bytes 131104 | tf_op jit(solution)/shard_map/all_to_all | solution.py:69
  132.1 7.2 %all-to-all-start.4 = ((f32[128,1,256]{2,1,0:T(1,128)}), f32[128,1,256]{2,1,0:T(1,128)S(1)}, u32[]{:S(2)}, u32[]{:S(2)}) async-start(f32[128,1,256]{2,1,0:T(1,128)} %copy.62), calls=%async_computation.4 | async-start | bytes 262144 | tf_op jit(solution)/shard_map/all_to_all | solution.py:68
  139.2 0.6 fusion.23
  139.9 0.6 convolution_add_fusion.3
  140.6 0.2 copy.65
  140.9 0.6 fusion.11
  141.4 13.8 %all-to-all-done.4 = f32[128,1,256]{2,1,0:T(1,128)S(1)} async-done(((f32[128,1,256]{2,1,0:T(1,128)}), f32[128,1,256]{2,1,0:T(1,128)S(1)}, u32[]{:S(2)}, u32[]{:S(2)}) %all-to-all-start.4) | async-done | bytes 131104 | tf_op jit(solution)/shard_map/all_to_all | solution.py:68
  155.2 0.6 convolution_subtract_fusion.3
  155.9 0.6 fusion.15
  156.5 0.6 convolution_add_fusion.2
  157.1 0.2 copy.66
  157.4 6.7 fusion.151
  164.1 8.4 %fusion.150 = f32[128,64,64]{2,1,0:T(8,128)} fusion(f32[128,64,4]{1,2,0:T(4,128)S(1)} %copy.65, f32[128,4,64]{2,1,0:T(4,128)S(1)} %copy.66), kind=kOutput, calls=%fused_computation.161 | convolution fusion | flops 25165824 | bytes 2359296 | tf_op jit(solution)/shard_map/kpm,kmr->kpr/dot_general | solution.py:30
  172.5 8.3 %convolution_subtract_fusion.2 = f32[128,64,64]{2,1,0:T(8,128)} fusion(f32[128,64,64]{2,1,0:T(8,128)S(1)} %fusion.151, f32[128,64,4]{1,2,0:T(4,128)S(1)} %copy.65, f32[128,4,64]{2,1,0:T(4,128)S(1)} %copy.70), kind=kOutput, calls=%fused_computation.7 | convolution fusion | flops 25690112 | bytes 4456448 | tf_op jit(solution)/shard_map/kpm,kmr->kpr/dot_general | solution.py:30
  180.8 3.8 copy.76
  184.6 9.8 %convolution_add_fusion.1 = f32[128,64,64]{2,1,0:T(8,128)} fusion(f32[128,64,64]{2,1,0:T(8,128)} %fusion.150, f32[128,64,4]{1,2,0:T(4,128)S(1)} %copy.69, f32[128,4,64]{2,1,0:T(4,128)S(1)} %copy.70), kind=kOutput, calls=%fused_computation.8 | convolution fusion | flops 25690112 | bytes 4456448 | tf_op jit(solution)/shard_map/kpm,kmr->kpr/dot_general | solution.py:30
  194.4 4.9 copy.71
  199.4 3.8 fusion.64
  203.2 2.3 fusion.3
  205.5 3.5 copy.77
  209.0 8.3 %all-to-all-start.6 = ((f32[128,1,4096]{2,1,0:T(1,128)}), f32[128,1,4096]{2,1,0:T(1,128)}, u32[]{:S(2)}, u32[]{:S(2)}) async-start(f32[128,1,4096]{2,1,0:T(1,128)} %copy.77), calls=%async_computation.6 | async-start | bytes 4194304 | tf_op jit(solution)/shard_map/all_to_all | solution.py:95
  217.2 3.8 fusion.70
  221.0 2.3 fusion.2
  223.4 3.5 copy.78
  226.8 85.7 %all-to-all-done.6 = f32[128,1,4096]{2,1,0:T(1,128)} async-done(((f32[128,1,4096]{2,1,0:T(1,128)}), f32[128,1,4096]{2,1,0:T(1,128)}, u32[]{:S(2)}, u32[]{:S(2)}) %all-to-all-start.6) | async-done | bytes 2097184 | tf_op jit(solution)/shard_map/all_to_all | solution.py:95
  312.6 11.3 %all-to-all-start.7 = ((f32[128,1,4096]{2,1,0:T(1,128)}), f32[128,1,4096]{2,1,0:T(1,128)S(1)}, u32[]{:S(2)}, u32[]{:S(2)}) async-start(f32[128,1,4096]{2,1,0:T(1,128)} %copy.78), calls=%async_computation.7 | async-start | bytes 4194304 | tf_op jit(solution)/shard_map/all_to_all | solution.py:102
  323.9 6.0 fusion.6
  329.9 89.8 %all-to-all-done.7 = f32[128,1,4096]{2,1,0:T(1,128)S(1)} async-done(((f32[128,1,4096]{2,1,0:T(1,128)}), f32[128,1,4096]{2,1,0:T(1,128)S(1)}, u32[]{:S(2)}, u32[]{:S(2)}) %all-to-all-start.7) | async-done | bytes 2097184 | tf_op jit(solution)/shard_map/all_to_all | solution.py:102
  419.7 4.9 fusion.1
  424.6 2.2 copy.79
  426.7 107.0 %all_to_all.65 = f32[128,1,4096]{2,1,0:T(1,128)S(1)} all-to-all(f32[128,1,4096]{2,1,0:T(1,128)S(1)} %copy.79), channel_id=1, replica_groups=mesh['tm'=128,'chan'=4] {'tm'}, dimensions={0} | all-to-all | bytes 4194304 | tf_op jit(solution)/shard_map/all_to_all | solution.py:111
  533.7 7.3 %reduce.6 = f32[128,4096]{1,0:T(8,128)} reduce(f32[128,1,4096]{2,1,0:T(1,128)S(1)} %all_to_all.65, f32[]{:T(128)} %constant.86), dimensions={1}, to_apply=%all_to_all.26.reduce_sub_computation | reduce | bytes 4194308 | tf_op jit(solution)/shard_map/all_to_all | solution.py:111
  541.0 4.8 reshape_reshape.11
  545.8 10.4 %fusion.152 = f32[64,64]{0,1:T(8,128)S(1)} fusion(f32[8192,64]{1,0:T(8,128)} %reshape_reshape.11), kind=kOutput, calls=%fused_computation.163 | convolution fusion | flops 402653184 | bytes 2113536 | tf_op jit(solution)/shard_map/nr,ns->rs/dot_general | solution.py:26
  556.2 104.1 %psum.7 = f32[64,64]{0,1:T(8,128)S(1)} all-reduce(f32[64,64]{0,1:T(8,128)S(1)} %fusion.152), channel_id=1, replica_groups=mesh['tm'=128,'chan'=4] {'tm','chan'}, use_global_device_ids=true, to_apply=%region_0.1 | all-reduce | flops 4096 | bytes 32768 | tf_op jit(solution)/shard_map/psum | solution.py:34
  660.5 5.8 cholesky.17
  666.3 0.6 compare_reduce_fusion
  667.0 0.7 fusion.77
  667.6 0.7 copy.83
  668.3 4.9 custom-call.7
  673.2 0.2 convolution_bitcast_fusion.2
  673.5 3.8 copy.80
  677.3 4.9 fusion.153
  (11 shorter events, 0.8 us)
Async XLA Ops:
  2.3 36.6 %all-to-all-start = ((f32[128,1,256]{2,1,0:T(1,128)}), f32[128,1,256]{2,1,0:T(1,128)S(1)}, u32[]{:S(2)}, u32[]{:S(2)}) async-start(f32[128,1,256]{2,1,0:T(1,128)} %copy.57), calls=%async_computation | async-start | bytes 262144 | tf_op jit(solution)/shard_map/all_to_all | solution.py:57
  38.8 23.2 %all-to-all-start.3 = ((f32[128,1,256]{2,1,0:T(1,128)}), f32[128,1,256]{2,1,0:T(1,128)S(1)}, u32[]{:S(2)}, u32[]{:S(2)}) async-start(f32[128,1,256]{2,1,0:T(1,128)} %copy.61), calls=%async_computation.3 | async-start | bytes 262144 | tf_op jit(solution)/shard_map/all_to_all | solution.py:58
  62.0 23.3 %all-to-all-start.2 = ((f32[128,1,256]{2,1,0:T(1,128)}), f32[128,1,256]{2,1,0:T(1,128)S(1)}, u32[]{:S(2)}, u32[]{:S(2)}) async-start(f32[128,1,256]{2,1,0:T(1,128)} %copy.59), calls=%async_computation.2 | async-start | bytes 262144 | tf_op jit(solution)/shard_map/all_to_all | solution.py:67
  85.2 23.2 %all-to-all-start.1 = ((f32[128,1,256]{2,1,0:T(1,128)}), f32[128,1,256]{2,1,0:T(1,128)S(1)}, u32[]{:S(2)}, u32[]{:S(2)}) async-start(f32[128,1,256]{2,1,0:T(1,128)} %copy.58), calls=%async_computation.1 | async-start | bytes 262144 | tf_op jit(solution)/shard_map/all_to_all | solution.py:66
  108.5 23.6 %all-to-all-start.5 = ((f32[128,1,256]{2,1,0:T(1,128)}), f32[128,1,256]{2,1,0:T(1,128)S(1)}, u32[]{:S(2)}, u32[]{:S(2)}) async-start(f32[128,1,256]{2,1,0:T(1,128)} %copy.63), calls=%async_computation.5 | async-start | bytes 262144 | tf_op jit(solution)/shard_map/all_to_all | solution.py:69
  132.1 23.1 %all-to-all-start.4 = ((f32[128,1,256]{2,1,0:T(1,128)}), f32[128,1,256]{2,1,0:T(1,128)S(1)}, u32[]{:S(2)}, u32[]{:S(2)}) async-start(f32[128,1,256]{2,1,0:T(1,128)} %copy.62), calls=%async_computation.4 | async-start | bytes 262144 | tf_op jit(solution)/shard_map/all_to_all | solution.py:68
  209.0 103.6 %all-to-all-start.6 = ((f32[128,1,4096]{2,1,0:T(1,128)}), f32[128,1,4096]{2,1,0:T(1,128)}, u32[]{:S(2)}, u32[]{:S(2)}) async-start(f32[128,1,4096]{2,1,0:T(1,128)} %copy.77), calls=%async_computation.6 | async-start | bytes 4194304 | tf_op jit(solution)/shard_map/all_to_all | solution.py:95
  312.6 107.1 %all-to-all-start.7 = ((f32[128,1,4096]{2,1,0:T(1,128)}), f32[128,1,4096]{2,1,0:T(1,128)S(1)}, u32[]{:S(2)}, u32[]{:S(2)}) async-start(f32[128,1,4096]{2,1,0:T(1,128)} %copy.78), calls=%async_computation.7 | async-start | bytes 4194304 | tf_op jit(solution)/shard_map/all_to_all | solution.py:102
where the time goes:
time: 692 us; the launch traced here: 683 us
  waiting for transfers between devices  261 us (38%)
  blocking collectives  211 us (30%)
  matrix products  78.4 us (11%)
  starting transfers between devices  76.6 us (11%)
  local copies, waits for them, and re-layouts  34.7 us (5%)
  other arithmetic  19.3 us (3%)
    all_to_all x1, blocking collectives, body(): lax.all_to_all(mixed, 'tm', split_axis=0, concat_axis=1, tiled=True)  107 us
    psum x1, blocking collectives, total_factor(): summed = lax.psum(gram_part, ('tm', 'chan'))  104 us
    all_to_all x1, waiting for transfers between devices, body(): lax.all_to_all(turned_im.reshape(shards, per_group, width), 'tm', split_a...  89.8 us
    all_to_all x1, waiting for transfers between devices, body(): lax.all_to_all(turned_re.reshape(shards, per_group, width), 'tm', split_a...  85.7 us
    dot_general x4, matrix products, product(): return jnp.einsum('kpm,kmr->kpr', left, right, precision=HIGHEST_PREC)  33.2 us
    dot_general x13, matrix products, plain_dot(): return jnp.dot(left, right, precision=HIGHEST_PREC)  21.6 us
    all_to_all x1, starting transfers between devices, body(): lax.all_to_all(markov_blocks, 'tm', split_axis=0, concat_axis=0, tiled=True)  20.6 us
    all_to_all x1, waiting for transfers between devices, body(): lax.all_to_all(spread[1], 'tm', split_axis=0, concat_axis=1, tiled=True)  14.7 us
  transfers between devices with their start and end apart: 8, of which 8 were waited for; matrix products, arithmetic and copies ran while one was open for 4% of the time, Pallas kernels for 0%

commit v1 on v0

--- a/solution.py
+++ b/solution.py
@@ -5,6 +5,12 @@
 from jax.sharding import PartitionSpec as P
 
 HIGHEST_PREC = lax.Precision.HIGHEST
+
+
+def gather_and_add(shard, axis):
+    parts = lax.all_gather(shard, axis, axis=0, tiled=False)
+    summed = parts.sum(axis=0)
+    return summed
 
 
 def circle(first, second, modulus):
@@ -31,7 +37,7 @@
 
 
 def total_factor(gram_part, row_total):
-    summed = lax.psum(gram_part, ("tm", "chan"))
+    summed = gather_and_add(gram_part, ("tm", "chan"))
     result = jnp.linalg.cholesky(summed / row_total)
     return result
 

time: 692 us -> 819 us (1.18)
  waiting for transfers between devices: 261 us -> 473 us
  blocking collectives: 211 us -> 107 us
  between operations: 1.41 us -> 14.9 us
    all_gather x0 -> x1, waiting for transfers between devices: none -> 212 us  [gather_and_add(): parts = lax.all_gather(shard, axis, axis=0, tiled=False)]
    psum x1 -> x0, blocking collectives: 104 us -> none  [total_factor(): summed = lax.psum(gram_part, ('tm', 'chan'))]
  transfers between devices with their start and end apart: 8 -> 9, of which waited for: 8 -> 9; matrix products, arithmetic and copies ran while one was open for 4% -> 4% of each run, Pallas kernels for 0% -> 0%
where the time goes in v1:
time: 819 us; the launch traced here: 810 us
  waiting for transfers between devices  473 us (58%)
  blocking collectives  107 us (13%)
  matrix products  77.5 us (9%)
  starting transfers between devices  76.5 us (9%)
  local copies, waits for them, and re-layouts  35 us (4%)
  other arithmetic  26.4 us (3%)
  between operations  14.9 us (2%)
    all_gather x1, waiting for transfers between devices, gather_and_add(): parts = lax.all_gather(shard, axis, axis=0, tiled=False)  212 us
    all_to_all x1, blocking collectives, body(): lax.all_to_all(mixed, 'tm', split_axis=0, concat_axis=1, tiled=True)  107 us
    all_to_all x1, waiting for transfers between devices, body(): lax.all_to_all(turned_im.reshape(shards, per_group, width), 'tm', split_a...  89.7 us
    all_to_all x1, waiting for transfers between devices, body(): lax.all_to_all(turned_re.reshape(shards, per_group, width), 'tm', split_a...  85.8 us
    dot_general x4, matrix products, product(): return jnp.einsum('kpm,kmr->kpr', left, right, precision=HIGHEST_PREC)  33.2 us
    all_to_all x1, starting transfers between devices, body(): lax.all_to_all(markov_blocks, 'tm', split_axis=0, concat_axis=0, tiled=True)  20.6 us
    dot_general x13, matrix products, plain_dot(): return jnp.dot(left, right, precision=HIGHEST_PREC)  20.1 us
  transfers between devices with their start and end apart: 9, of which 9 were waited for; matrix products, arithmetic and copies ran while one was open for 4% of the time, Pallas kernels for 0%

profile of v1, /device:TPU:1, one launch (start us, length us, event | category | flops | bytes accessed | tf_op | source)
XLA Modules:
  0.0 810.3 jit_solution(5839791852053315633)
XLA Ops:
  7.2 1.7 copy.54
  8.8 20.6 %all-to-all-start = ((f32[128,1,256]{2,1,0:T(1,128)}), f32[128,1,256]{2,1,0:T(1,128)S(1)}, u32[]{:S(2)}, u32[]{:S(2)}) async-start(f32[128,1,256]{2,1,0:T(1,128)} %copy.54), calls=%async_computation | async-start | bytes 262144 | tf_op jit(solution)/shard_map/all_to_all | solution.py:63
  29.4 1.7 copy.58
  31.0 14.3 %all-to-all-done = f32[128,1,256]{2,1,0:T(1,128)S(1)} async-done(((f32[128,1,256]{2,1,0:T(1,128)}), f32[128,1,256]{2,1,0:T(1,128)S(1)}, u32[]{:S(2)}, u32[]{:S(2)}) %all-to-all-start) | async-done | bytes 131104 | tf_op jit(solution)/shard_map/all_to_all | solution.py:63
  45.4 7.2 all-to-all-start.3
  52.6 0.5 fusion.10
  53.1 0.8 copy.56
  53.9 14.7 %all-to-all-done.3 = f32[128,1,256]{2,1,0:T(1,128)S(1)} async-done(((f32[128,1,256]{2,1,0:T(1,128)}), f32[128,1,256]{2,1,0:T(1,128)S(1)}, u32[]{:S(2)}, u32[]{:S(2)}) %all-to-all-start.3) | async-done | bytes 131104 | tf_op jit(solution)/shard_map/all_to_all | solution.py:64
  68.6 7.2 all-to-all-start.2
  75.8 0.5 convolution_bitcast_fusion.1
  76.3 0.8 copy.55
  77.1 14.7 %all-to-all-done.2 = f32[128,1,256]{2,1,0:T(1,128)S(1)} async-done(((f32[128,1,256]{2,1,0:T(1,128)}), f32[128,1,256]{2,1,0:T(1,128)S(1)}, u32[]{:S(2)}, u32[]{:S(2)}) %all-to-all-start.2) | async-done | bytes 131104 | tf_op jit(solution)/shard_map/all_to_all | solution.py:73
  91.8 7.2 all-to-all-start.1
  99.0 0.5 fusion.9
  99.5 0.8 copy.60
  100.3 14.7 %all-to-all-done.1 = f32[128,1,256]{2,1,0:T(1,128)S(1)} async-done(((f32[128,1,256]{2,1,0:T(1,128)}), f32[128,1,256]{2,1,0:T(1,128)S(1)}, u32[]{:S(2)}, u32[]{:S(2)}) %all-to-all-start.1) | async-done | bytes 131104 | tf_op jit(solution)/shard_map/all_to_all | solution.py:72
  115.0 7.7 all-to-all-start.5
  122.7 0.5 convolution_bitcast_fusion
  123.2 0.8 copy.59
  124.0 0.6 fusion.19
  124.5 0.6 convolution_subtract_fusion.4
  125.1 13.5 %all-to-all-done.5 = f32[128,1,256]{2,1,0:T(1,128)S(1)} async-done(((f32[128,1,256]{2,1,0:T(1,128)}), f32[128,1,256]{2,1,0:T(1,128)S(1)}, u32[]{:S(2)}, u32[]{:S(2)}) %all-to-all-start.5) | async-done | bytes 131104 | tf_op jit(solution)/shard_map/all_to_all | solution.py:75
  138.6 7.2 all-to-all-start.4
  145.8 0.6 fusion.23
  146.4 0.6 convolution_add_fusion.3
  147.4 0.6 fusion.11
  148.0 13.8 %all-to-all-done.4 = f32[128,1,256]{2,1,0:T(1,128)S(1)} async-done(((f32[128,1,256]{2,1,0:T(1,128)}), f32[128,1,256]{2,1,0:T(1,128)S(1)}, u32[]{:S(2)}, u32[]{:S(2)}) %all-to-all-start.4) | async-done | bytes 131104 | tf_op jit(solution)/shard_map/all_to_all | solution.py:74
  161.8 0.6 convolution_subtract_fusion.3
  162.4 0.6 fusion.15
  163.0 0.6 convolution_add_fusion.2
  164.0 6.7 fusion.151
  170.7 8.4 %fusion.150 = f32[128,64,64]{2,1,0:T(8,128)} fusion(f32[128,64,4]{1,2,0:T(4,128)S(1)} %copy.62, f32[128,4,64]{2,1,0:T(4,128)S(1)} %copy.63), kind=kOutput, calls=%fused_computation.160 | convolution fusion | flops 25165824 | bytes 2359296 | tf_op jit(solution)/shard_map/kpm,kmr->kpr/dot_general | solution.py:36
  179.1 8.3 %convolution_subtract_fusion.2 = f32[128,64,64]{2,1,0:T(8,128)} fusion(f32[128,64,64]{2,1,0:T(8,128)S(1)} %fusion.151, f32[128,64,4]{1,2,0:T(4,128)S(1)} %copy.62, f32[128,4,64]{2,1,0:T(4,128)S(1)} %copy.67), kind=kOutput, calls=%fused_computation.7 | convolution fusion | flops 25690112 | bytes 4456448 | tf_op jit(solution)/shard_map/kpm,kmr->kpr/dot_general | solution.py:36
  187.4 3.8 copy.73
  191.2 9.8 %convolution_add_fusion.1 = f32[128,64,64]{2,1,0:T(8,128)} fusion(f32[128,64,64]{2,1,0:T(8,128)} %fusion.150, f32[128,64,4]{1,2,0:T(4,128)S(1)} %copy.66, f32[128,4,64]{2,1,0:T(4,128)S(1)} %copy.67), kind=kOutput, calls=%fused_computation.8 | convolution fusion | flops 25690112 | bytes 4456448 | tf_op jit(solution)/shard_map/kpm,kmr->kpr/dot_general | solution.py:36
  201.0 4.9 copy.68
  205.9 3.8 fusion.64
  209.7 2.3 fusion.3
  212.1 3.5 copy.74
  215.5 8.2 %all-to-all-start.6 = ((f32[128,1,4096]{2,1,0:T(1,128)}), f32[128,1,4096]{2,1,0:T(1,128)}, u32[]{:S(2)}, u32[]{:S(2)}) async-start(f32[128,1,4096]{2,1,0:T(1,128)} %copy.74), calls=%async_computation.6 | async-start | bytes 4194304 | tf_op jit(solution)/shard_map/all_to_all | solution.py:101
  223.8 3.8 fusion.70
  227.6 2.3 fusion.2
  229.9 3.5 copy.75
  233.4 85.8 %all-to-all-done.6 = f32[128,1,4096]{2,1,0:T(1,128)} async-done(((f32[128,1,4096]{2,1,0:T(1,128)}), f32[128,1,4096]{2,1,0:T(1,128)}, u32[]{:S(2)}, u32[]{:S(2)}) %all-to-all-start.6) | async-done | bytes 2097184 | tf_op jit(solution)/shard_map/all_to_all | solution.py:101
  319.2 11.0 %all-to-all-start.7 = ((f32[128,1,4096]{2,1,0:T(1,128)}), f32[128,1,4096]{2,1,0:T(1,128)S(1)}, u32[]{:S(2)}, u32[]{:S(2)}) async-start(f32[128,1,4096]{2,1,0:T(1,128)} %copy.75), calls=%async_computation.7 | async-start | bytes 4194304 | tf_op jit(solution)/shard_map/all_to_all | solution.py:108
  330.2 0.2 all-gather.3.cloned.1.call-start
  330.4 6.0 fusion.6
  336.4 89.7 %all-to-all-done.7 = f32[128,1,4096]{2,1,0:T(1,128)S(1)} async-done(((f32[128,1,4096]{2,1,0:T(1,128)}), f32[128,1,4096]{2,1,0:T(1,128)S(1)}, u32[]{:S(2)}, u32[]{:S(2)}) %all-to-all-start.7) | async-done | bytes 2097184 | tf_op jit(solution)/shard_map/all_to_all | solution.py:108
  426.1 4.9 fusion.1
  431.0 2.2 copy.76
  433.2 107.0 %all_to_all.65 = f32[128,1,4096]{2,1,0:T(1,128)S(1)} all-to-all(f32[128,1,4096]{2,1,0:T(1,128)S(1)} %copy.76), channel_id=1, replica_groups=mesh['tm'=128,'chan'=4] {'tm'}, dimensions={0} | all-to-all | bytes 4194304 | tf_op jit(solution)/shard_map/all_to_all | solution.py:117
  540.1 7.3 reduce.6
  547.4 4.8 reshape_reshape.11
  552.2 11.1 %fusion.152 = f32[64,64]{1,0:T(8,128)} fusion(f32[8192,64]{1,0:T(8,128)} %reshape_reshape.11), kind=kOutput, calls=%fused_computation.162 | convolution fusion | flops 402653184 | bytes 2113536 | tf_op jit(solution)/shard_map/nr,ns->rs/dot_general | solution.py:32
  563.3 4.1 copy.77
  567.4 212.0 %all-gather.3.cloned.1.call-done = f32[32768,64]{1,0:T(8,128)} async-done(((f32[64,64]{1,0:T(8,128)}), f32[32768,64]{1,0:T(8,128)}) %all-gather.3.cloned.1.call-update) | async-done | bytes 8388624 | tf_op jit(solution)/shard_map/all_gather | solution.py:11
  779.5 7.1 reduce_sum.11
  786.6 5.8 cholesky.17
  792.5 0.6 compare_reduce_fusion
  793.2 0.7 fusion.77
  793.8 0.7 copy.79
  794.5 4.9 custom-call.7
  799.4 0.2 convolution_bitcast_fusion.2
  799.7 3.3 fusion.153
  (15 shorter events, 1.1 us)
Async XLA Ops:
  8.8 36.6 %all-to-all-start = ((f32[128,1,256]{2,1,0:T(1,128)}), f32[128,1,256]{2,1,0:T(1,128)S(1)}, u32[]{:S(2)}, u32[]{:S(2)}) async-start(f32[128,1,256]{2,1,0:T(1,128)} %copy.54), calls=%async_computation | async-start | bytes 262144 | tf_op jit(solution)/shard_map/all_to_all | solution.py:63
  45.4 23.2 %all-to-all-start.3 = ((f32[128,1,256]{2,1,0:T(1,128)}), f32[128,1,256]{2,1,0:T(1,128)S(1)}, u32[]{:S(2)}, u32[]{:S(2)}) async-start(f32[128,1,256]{2,1,0:T(1,128)} %copy.58), calls=%async_computation.3 | async-start | bytes 262144 | tf_op jit(solution)/shard_map/all_to_all | solution.py:64
  68.6 23.2 %all-to-all-start.2 = ((f32[128,1,256]{2,1,0:T(1,128)}), f32[128,1,256]{2,1,0:T(1,128)S(1)}, u32[]{:S(2)}, u32[]{:S(2)}) async-start(f32[128,1,256]{2,1,0:T(1,128)} %copy.56), calls=%async_computation.2 | async-start | bytes 262144 | tf_op jit(solution)/shard_map/all_to_all | solution.py:73
  91.8 23.2 %all-to-all-start.1 = ((f32[128,1,256]{2,1,0:T(1,128)}), f32[128,1,256]{2,1,0:T(1,128)S(1)}, u32[]{:S(2)}, u32[]{:S(2)}) async-start(f32[128,1,256]{2,1,0:T(1,128)} %copy.55), calls=%async_computation.1 | async-start | bytes 262144 | tf_op jit(solution)/shard_map/all_to_all | solution.py:72
  115.0 23.6 %all-to-all-start.5 = ((f32[128,1,256]{2,1,0:T(1,128)}), f32[128,1,256]{2,1,0:T(1,128)S(1)}, u32[]{:S(2)}, u32[]{:S(2)}) async-start(f32[128,1,256]{2,1,0:T(1,128)} %copy.60), calls=%async_computation.5 | async-start | bytes 262144 | tf_op jit(solution)/shard_map/all_to_all | solution.py:75
  138.6 23.2 %all-to-all-start.4 = ((f32[128,1,256]{2,1,0:T(1,128)}), f32[128,1,256]{2,1,0:T(1,128)S(1)}, u32[]{:S(2)}, u32[]{:S(2)}) async-start(f32[128,1,256]{2,1,0:T(1,128)} %copy.59), calls=%async_computation.4 | async-start | bytes 262144 | tf_op jit(solution)/shard_map/all_to_all | solution.py:74
  215.5 103.6 %all-to-all-start.6 = ((f32[128,1,4096]{2,1,0:T(1,128)}), f32[128,1,4096]{2,1,0:T(1,128)}, u32[]{:S(2)}, u32[]{:S(2)}) async-start(f32[128,1,4096]{2,1,0:T(1,128)} %copy.74), calls=%async_computation.6 | async-start | bytes 4194304 | tf_op jit(solution)/shard_map/all_to_all | solution.py:101
  319.2 107.0 %all-to-all-start.7 = ((f32[128,1,4096]{2,1,0:T(1,128)}), f32[128,1,4096]{2,1,0:T(1,128)S(1)}, u32[]{:S(2)}, u32[]{:S(2)}) async-start(f32[128,1,4096]{2,1,0:T(1,128)} %copy.75), calls=%async_computation.7 | async-start | bytes 4194304 | tf_op jit(solution)/shard_map/all_to_all | solution.py:108
  330.2 449.2 %all-gather.3.cloned.1.call-start = ((), (), s32[]{:S(2)}) async-start(), calls=%async_computation.9 | async-start | bytes 16809984 | tf_op jit(solution)/shard_map/all_gather | solution.py:11
  779.5 20.2 %copy-start = (f32[128,1,4096]{0,2,1:T(8,128)S(1)}, f32[128,1,4096]{0,2,1:T(8,128)}, u32[]{:S(2)}) copy-start(f32[128,1,4096]{0,2,1:T(8,128)} %copy.77) | copy-start | bytes 6291460
Sparse Core Ops, SparseCore 0:
  563.5 215.9 all-gather.2
